TPU v7x, 256 devices: a whole 4x4x8 slice. The times are simulated.
256 devices in a mesh: shard: 8 (over y, core), tensor: 4 (over x), section: 8 (over z).
Axes of the slice: x: 4, y: 4, z: 8, core: 2. Of those that a mesh axis runs over, the one named last changes fastest.
Arguments:
- normed_inputs: bfloat16 [65536, 4096], P(('shard', 'section')), may hold values from -320 to 320
- projection_cotangent: bfloat16 [65536, 2, 1024], P(('shard', 'section'), None, 'tensor'), may hold values from -1 to 1
- small_partials: bfloat16 [64, 10, 4096], P(('shard', 'section'), None, 'tensor'), may hold values from -2000 to 2000
- master_weights: float32 [4096, 2, 1024], P(('shard', 'section'), None, 'tensor'), may hold values from -4 to 4
- first_moment: float32 [4096, 2, 1024], P(('shard', 'section'), None, 'tensor'), may hold values from -3 to 3
- second_moment: float32 [4096, 2, 1024], P(('shard', 'section'), None, 'tensor'), may hold values from 0.05 to 1
- small_master: float32 [10, 4096], P(None, 'tensor'), may hold values from -4 to 4
- small_first: float32 [10, 4096], P(None, 'tensor'), may hold values from -3 to 3
- small_second: float32 [10, 4096], P(None, 'tensor'), may hold values from 0.05 to 1
Outputs:
- updated_master: float32 [4096, 2, 1024], P(('shard', 'section'), None, 'tensor')
- updated_first: float32 [4096, 2, 1024], P(('shard', 'section'), None, 'tensor')
- updated_second: float32 [4096, 2, 1024], P(('shard', 'section'), None, 'tensor')
- gathered_weights: bfloat16 [4096, 2, 1024], P(None, None, 'tensor')
- small_updated_master: float32 [10, 4096], P(None, 'tensor')
- small_updated_first: float32 [10, 4096], P(None, 'tensor')
- small_updated_second: float32 [10, 4096], P(None, 'tensor')
- small_weights: bfloat16 [10, 4096], P(None, 'tensor')
All inputs are finite; a program needn't handle non-finite values.
Results may differ from a plain program's by a relative error of at most 0.0015.
Values may be sent and summed in bfloat16 or wider, within the bound.
A program may use at most 64 MiB of HBM per device.

v0:
```python
import math
import jax
import jax.numpy as jnp
from jax import lax
from jax.sharding import PartitionSpec as P

D = 4096
EXPERTS = 8
STEP = 10
KV_COLS = 1024
SMALL_ROWS = 10
beta_one = 0.9
beta_two = 0.95
learning_rate = 0.01
weight_decay = 0.1
epsilon = 1e-08
clip_factor = 0.5


def adamw(gradient, scale, first, second, master, decay):
    clipped = gradient * scale
    first_new = beta_one * first + (1.0 - beta_one) * clipped
    second_new = beta_two * second + (1.0 - beta_two) * clipped * clipped
    first_hat = first_new / (1.0 - beta_one**STEP)
    second_hat = second_new / (1.0 - beta_two**STEP)
    master_new = master - learning_rate * (
        first_hat / (jnp.sqrt(second_hat) + epsilon) + decay * master
    )
    return (master_new, first_new, second_new)


def body(
    normed_inputs,
    projection_cotangent,
    small_partials,
    master_weights,
    first_moment,
    second_moment,
    small_master,
    small_first,
    small_second,
):
    gradient = lax.psum_scatter(
        jnp.einsum(
            "tf,tjc->fjc", normed_inputs, projection_cotangent, preferred_element_type=jnp.float32
        ),
        ("shard", "section"),
        scatter_dimension=0,
        tiled=True,
    )
    owned_squares = jnp.sum(gradient * gradient)
    local_small = small_partials[0].astype(jnp.float32)
    small_gradient = lax.psum(local_small, ("shard", "section"))
    big_total = lax.psum(owned_squares, ("shard", "tensor", "section"))
    small_total = lax.psum(jnp.sum(small_gradient * small_gradient), "tensor")
    total = big_total + small_total
    limit = clip_factor * math.sqrt(2 * D * KV_COLS + SMALL_ROWS * D)
    scale = jnp.minimum(1.0, limit / (jnp.sqrt(total) + 1e-06))
    master_new, first_new, second_new = adamw(
        gradient, scale, first_moment, second_moment, master_weights, weight_decay
    )
    row_decay = jnp.where(jnp.arange(SMALL_ROWS)[:, None] < EXPERTS, weight_decay, 0.0).astype(
        jnp.float32
    )
    small_master_new, small_first_new, small_second_new = adamw(
        small_gradient, scale, small_first, small_second, small_master, row_decay
    )
    owned_weights = master_new.astype(jnp.bfloat16)
    gathered = lax.all_gather(owned_weights, ("shard", "section"), axis=0, tiled=True)
    return (
        master_new,
        first_new,
        second_new,
        gathered,
        small_master_new,
        small_first_new,
        small_second_new,
        small_master_new.astype(jnp.bfloat16),
    )


def solution(mesh):
    placed = (
        P(("shard", "section"), None),
        P(("shard", "section"), None, "tensor"),
        P(("shard", "section"), None, "tensor"),
        P(("shard", "section"), None, "tensor"),
        P(("shard", "section"), None, "tensor"),
        P(("shard", "section"), None, "tensor"),
        P(None, "tensor"),
        P(None, "tensor"),
        P(None, "tensor"),
    )
    return jax.shard_map(
        body,
        mesh=mesh,
        in_specs=placed,
        out_specs=(
            P(("shard", "section"), None, "tensor"),
            P(("shard", "section"), None, "tensor"),
            P(("shard", "section"), None, "tensor"),
            P(None, None, "tensor"),
            P(None, "tensor"),
            P(None, "tensor"),
            P(None, "tensor"),
            P(None, "tensor"),
        ),
        check_vma=False,
    )
```

profile of v0, /device:TPU:1, one launch (start us, length us, event | category | flops | bytes accessed | tf_op | source)
XLA Modules:
  0.0 454.1 jit_solution(6464595801956574734)
XLA Ops:
  7.2 0.0 copy-start
  7.2 0.0 reduce-scatter.2.cloned.1.call-start
  7.2 1.2 copy-done
  8.4 10.3 %fusion = f32[4096,2,256]{2,0,1:T(8,128)} fusion(bf16[1024,4096]{1,0:T(8,128)(2,1)} %param.9, bf16[1024,2,256]{2,1,0:T(2,128)(2,1)S(1)} %copy-done), kind=kOutput, calls=%fused_computation | convolution fusion | flops 4294967296 | bytes 17825792 | tf_op jit(solution)/shard_map/tf,tjc->fjc/dot_general | solution.py:44
  18.8 0.0 copy-start.4
  18.8 0.0 copy-start.5
  18.8 0.0 copy-start.6
  18.8 0.0 reduce-scatter.2.cloned.1.call-update
  18.8 0.0 all-gather.2.cloned.1.call-start
  18.9 0.6 copy-done.7
  19.5 246.8 %psum.22 = f32[10,1024]{1,0:T(8,128)S(1)} all-reduce(f32[10,1024]{1,0:T(8,128)S(1)} %bitcast_convert_fusion), channel_id=1, replica_groups=mesh['shard'=8,'tensor'=4,'section'=8] {'shard','section'}, use_global_device_ids=true, to_apply=%region_3.0 | all-reduce | flops 10240 | bytes 81920 | tf_op jit(solution)/shard_map/psum | solution.py:53
  266.3 0.6 multiply_reduce_fusion.1
  266.9 1.5 multiply_reduce_fusion
  268.4 9.4 %psum.23 = f32[]{:T(128)} all-reduce(f32[]{:T(128)} %multiply_reduce_fusion.1), channel_id=1, replica_groups=mesh['shard'=8,'tensor'=4,'section'=8] {'tensor'}, use_global_device_ids=true, to_apply=%region_5.0 | all-reduce | flops 1 | bytes 8 | tf_op jit(solution)/shard_map/psum | solution.py:55
  277.9 81.1 %psum.21 = f32[]{:T(128)} all-reduce(f32[]{:T(128)} %multiply_reduce_fusion), channel_id=1, replica_groups=mesh['shard'=8,'tensor'=4,'section'=8] {'shard','tensor','section'}, use_global_device_ids=true, to_apply=%region_2.0 | all-reduce | flops 1 | bytes 8 | tf_op jit(solution)/shard_map/psum | solution.py:54
  360.4 1.7 fusion.8
  362.1 0.0 all-gather.2.cloned.1.call-update
  362.1 0.8 copy.23
  362.9 0.8 copy.24
  363.6 0.8 copy.25
  364.4 0.0 copy-done.5
  364.4 0.7 fusion.6
  365.1 72.0 %all-gather.2.cloned.1.call-done = bf16[4096,2,256]{2,0,1:T(8,128)(2,1)} async-done(((bf16[64,2,256]{2,0,1:T(8,128)(2,1)}), bf16[4096,2,256]{2,0,1:T(8,128)(2,1)}) %all-gather.2.cloned.1.call-update) | async-done | bytes 4194320 | tf_op jit(solution)/shard_map/all_gather | solution.py:69
  437.1 10.1 %copy.26 = bf16[4096,2,256]{2,1,0:T(2,128)(2,1)} copy(bf16[4096,2,256]{2,0,1:T(8,128)(2,1)} %all-gather.2.cloned.1.call-done) | data formatting | bytes 8388608
  (12 shorter events, 0.0 us)
Async XLA Ops:
  7.2 1.2 copy-start
  7.2 259.7 %reduce-scatter.2.cloned.1.call-start = ((), (), s32[]{:S(2)}) async-start(), calls=%async_computation.1 | async-start | bytes 8519680 | tf_op jit(solution)/shard_map/reduce_scatter | solution.py:43
  18.7 0.8 copy-start.7
  18.7 341.7 %copy-start.1 = (f32[64,2,256]{2,1,0:T(2,128)S(1)}, f32[64,2,256]{2,1,0:T(2,128)}, u32[]{:S(2)}) copy-start(f32[64,2,256]{2,1,0:T(2,128)} %param.12) | copy-start | bytes 393220
  18.7 341.7 %copy-start.2 = (f32[64,2,256]{2,1,0:T(2,128)S(1)}, f32[64,2,256]{2,1,0:T(2,128)}, u32[]{:S(2)}) copy-start(f32[64,2,256]{2,1,0:T(2,128)} %param.13) | copy-start | bytes 393220
  18.8 341.7 %copy-start.3 = (f32[64,2,256]{2,1,0:T(2,128)S(1)}, f32[64,2,256]{2,1,0:T(2,128)}, u32[]{:S(2)}) copy-start(f32[64,2,256]{2,1,0:T(2,128)} %param.14) | copy-start | bytes 393220
  18.8 345.6 %copy-start.4 = (f32[10,1024]{1,0:T(8,128)S(1)}, f32[10,1024]{1,0:T(8,128)}, u32[]{:S(2)}) copy-start(f32[10,1024]{1,0:T(8,128)} %param.15) | copy-start | bytes 122884
  18.8 345.6 %copy-start.5 = (f32[10,1024]{1,0:T(8,128)S(1)}, f32[10,1024]{1,0:T(8,128)}, u32[]{:S(2)}) copy-start(f32[10,1024]{1,0:T(8,128)} %param.16) | copy-start | bytes 122884
  18.8 345.6 %copy-start.6 = (f32[10,1024]{1,0:T(8,128)S(1)}, f32[10,1024]{1,0:T(8,128)}, u32[]{:S(2)}) copy-start(f32[10,1024]{1,0:T(8,128)} %param.17) | copy-start | bytes 122884
  18.8 418.3 %all-gather.2.cloned.1.call-start = ((), (), s32[]{:S(2)}) async-start(), calls=%async_computation.2 | async-start | bytes 4259840 | tf_op jit(solution)/shard_map/all_gather | solution.py:69
Sparse Core Ops, SparseCore 0:
  18.9 150.9 reduce-scatter.1
  362.2 74.8 all-gather.1
where the time goes:
time: 455 us; the launch traced here: 454 us
  blocking collectives  337 us (74%)
  waiting for transfers between devices  72 us (16%)
  between operations  15.5 us (3%)
  local copies, waits for them, and re-layouts  14.2 us (3%)
  matrix products  10.3 us (2%)
    psum x1, blocking collectives, body(): small_gradient = lax.psum(local_small, ('shard', 'section'))  247 us
    psum x1, blocking collectives, body(): big_total = lax.psum(owned_squares, ('shard', 'tensor', 'section'))  81.1 us
    all_gather x1, waiting for transfers between devices, body(): lax.all_gather(owned_weights, ('shard', 'section'), axis=0, tiled=True)  72 us
    unnamed x20, local copies, waits for them, and re-layouts  14.2 us
    dot_general x1, matrix products, body(): jnp.einsum('tf,tjc->fjc', normed_inputs, projection_cotangent, preferred_...  10.3 us
    psum x1, blocking collectives, body(): small_total = lax.psum(jnp.sum(small_gradient * small_gradient), 'tensor')  9.45 us
  transfers between devices with their start and end apart: 2, of which 1 were waited for; matrix products, arithmetic and copies ran while one was open for 1% of the time, Pallas kernels for 0%

commit v1 on v0

--- a/solution.py
+++ b/solution.py
@@ -50,7 +50,8 @@
     )
     owned_squares = jnp.sum(gradient * gradient)
     local_small = small_partials[0].astype(jnp.float32)
-    small_gradient = lax.psum(local_small, ("shard", "section"))
+    all_rows = lax.psum(local_small, "section")
+    small_gradient = lax.psum(all_rows, "shard")
     big_total = lax.psum(owned_squares, ("shard", "tensor", "section"))
     small_total = lax.psum(jnp.sum(small_gradient * small_gradient), "tensor")
     total = big_total + small_total

time: 455 us -> 357 us (0.78)
  blocking collectives: 337 us -> 145 us
  waiting for transfers between devices: 72 us -> 166 us
    psum x1 -> x2, blocking collectives: 247 us -> 55.6 us  [the longest x1 28.7 us: body(): small_gradient = lax.psum(all_rows, 'shard')]
    reduce_scatter x1, waiting for transfers between devices: 0.01 us -> 93.6 us  [body(): lax.psum_scatter(jnp.einsum('tf,tjc->fjc', normed_inputs, projection_cota...]
  transfers between devices with their start and end apart: 2 -> 2, of which waited for: 1 -> 2; matrix products, arithmetic and copies ran while one was open for 1% -> 1% of each run, Pallas kernels for 0% -> 0%
where the time goes in v1:
time: 357 us; the launch traced here: 356 us
  waiting for transfers between devices  166 us (46%)
  blocking collectives  145 us (41%)
  between operations  15.5 us (4%)
  local copies, waits for them, and re-layouts  14.2 us (4%)
  matrix products  10.3 us (3%)
  other arithmetic  4.55 us (1%)
    reduce_scatter x1, waiting for transfers between devices, body(): lax.psum_scatter(jnp.einsum('tf,tjc->fjc', normed_inputs, projection_cota...  93.6 us
    psum x1, blocking collectives, body(): big_total = lax.psum(owned_squares, ('shard', 'tensor', 'section'))  81 us
    all_gather x1, waiting for transfers between devices, body(): lax.all_gather(owned_weights, ('shard', 'section'), axis=0, tiled=True)  72.4 us
    psum x1, blocking collectives, body(): small_gradient = lax.psum(all_rows, 'shard')  28.7 us
    psum x1, blocking collectives, body(): all_rows = lax.psum(local_small, 'section')  26.9 us
    unnamed x20, local copies, waits for them, and re-layouts  14.2 us
    dot_general x1, matrix products, body(): jnp.einsum('tf,tjc->fjc', normed_inputs, projection_cotangent, preferred_...  10.3 us
    psum x1, blocking collectives, body(): small_total = lax.psum(jnp.sum(small_gradient * small_gradient), 'tensor')  8.62 us
  transfers between devices with their start and end apart: 2, of which 2 were waited for; matrix products, arithmetic and copies ran while one was open for 1% of the time, Pallas kernels for 0%

profile of v1, /device:TPU:1, one launch (start us, length us, event | category | flops | bytes accessed | tf_op | source)
XLA Modules:
  0.0 356.0 jit_solution(14598114963233659306)
XLA Ops:
  7.2 0.0 copy-start
  7.2 0.0 reduce-scatter.2.cloned.1.call-start
  7.2 1.2 copy-done
  8.4 10.3 %fusion = f32[4096,2,256]{2,0,1:T(8,128)} fusion(bf16[1024,4096]{1,0:T(8,128)(2,1)} %param.9, bf16[1024,2,256]{2,1,0:T(2,128)(2,1)S(1)} %copy-done), kind=kOutput, calls=%fused_computation | convolution fusion | flops 4294967296 | bytes 17825792 | tf_op jit(solution)/shard_map/tf,tjc->fjc/dot_general | solution.py:44
  18.8 0.0 copy-start.5
  18.8 0.0 copy-start.6
  18.8 0.0 reduce-scatter.2.cloned.1.call-update
  18.8 0.0 all-gather.2.cloned.1.call-start
  18.9 0.6 copy-done.7
  19.5 26.9 %psum.29 = f32[10,1024]{1,0:T(8,128)S(1)} all-reduce(f32[10,1024]{1,0:T(8,128)S(1)} %bitcast_convert_fusion), channel_id=1, replica_groups=mesh['shard'=8,'tensor'=4,'section'=8] {'section'}, use_global_device_ids=true, to_apply=%region_3.0 | all-reduce | flops 10240 | bytes 81920 | tf_op jit(solution)/shard_map/psum | solution.py:53
  46.5 28.7 %psum.30 = f32[10,1024]{1,0:T(8,128)S(1)} all-reduce(f32[10,1024]{1,0:T(8,128)S(1)} %psum.29), channel_id=1, replica_groups=mesh['shard'=8,'tensor'=4,'section'=8] {'shard'}, use_global_device_ids=true, to_apply=%region_4.0 | all-reduce | flops 10240 | bytes 81920 | tf_op jit(solution)/shard_map/psum | solution.py:54
  75.1 0.6 multiply_reduce_fusion.1
  75.8 93.6 %reduce-scatter.2.cloned.1.call-done = f32[64,2,256]{2,0,1:T(8,128)} async-done(((f32[4096,2,256]{2,0,1:T(8,128)}), f32[64,2,256]{2,0,1:T(8,128)}) %reduce-scatter.2.cloned.1.call-update) | async-done | bytes 131088 | tf_op jit(solution)/shard_map/reduce_scatter | solution.py:43
  169.4 1.5 multiply_reduce_fusion
  170.9 8.6 %psum.31 = f32[]{:T(128)} all-reduce(f32[]{:T(128)} %multiply_reduce_fusion.1), channel_id=1, replica_groups=mesh['shard'=8,'tensor'=4,'section'=8] {'tensor'}, use_global_device_ids=true, to_apply=%region_6.0 | all-reduce | flops 1 | bytes 8 | tf_op jit(solution)/shard_map/psum | solution.py:56
  179.6 81.0 %psum.28 = f32[]{:T(128)} all-reduce(f32[]{:T(128)} %multiply_reduce_fusion), channel_id=1, replica_groups=mesh['shard'=8,'tensor'=4,'section'=8] {'shard','tensor','section'}, use_global_device_ids=true, to_apply=%region_2.0 | all-reduce | flops 1 | bytes 8 | tf_op jit(solution)/shard_map/psum | solution.py:55
  261.9 1.7 fusion.8
  263.6 0.0 all-gather.2.cloned.1.call-update
  263.6 0.8 copy.23
  264.4 0.8 copy.24
  265.1 0.8 copy.25
  265.9 0.7 fusion.6
  266.6 72.4 %all-gather.2.cloned.1.call-done = bf16[4096,2,256]{2,0,1:T(8,128)(2,1)} async-done(((bf16[64,2,256]{2,0,1:T(8,128)(2,1)}), bf16[4096,2,256]{2,0,1:T(8,128)(2,1)}) %all-gather.2.cloned.1.call-update) | async-done | bytes 4194320 | tf_op jit(solution)/shard_map/all_gather | solution.py:70
  339.0 10.1 %copy.26 = bf16[4096,2,256]{2,1,0:T(2,128)(2,1)} copy(bf16[4096,2,256]{2,0,1:T(8,128)(2,1)} %all-gather.2.cloned.1.call-done) | data formatting | bytes 8388608
  (13 shorter events, 0.0 us)
Async XLA Ops:
  7.2 1.2 copy-start
  7.2 162.2 %reduce-scatter.2.cloned.1.call-start = ((), (), s32[]{:S(2)}) async-start(), calls=%async_computation.1 | async-start | bytes 8519680 | tf_op jit(solution)/shard_map/reduce_scatter | solution.py:43
  18.7 0.8 copy-start.7
  18.7 243.2 %copy-start.1 = (f32[64,2,256]{2,1,0:T(2,128)S(1)}, f32[64,2,256]{2,1,0:T(2,128)}, u32[]{:S(2)}) copy-start(f32[64,2,256]{2,1,0:T(2,128)} %param.12) | copy-start | bytes 393220
  18.7 243.2 %copy-start.2 = (f32[64,2,256]{2,1,0:T(2,128)S(1)}, f32[64,2,256]{2,1,0:T(2,128)}, u32[]{:S(2)}) copy-start(f32[64,2,256]{2,1,0:T(2,128)} %param.13) | copy-start | bytes 393220
  18.8 243.2 %copy-start.3 = (f32[64,2,256]{2,1,0:T(2,128)S(1)}, f32[64,2,256]{2,1,0:T(2,128)}, u32[]{:S(2)}) copy-start(f32[64,2,256]{2,1,0:T(2,128)} %param.14) | copy-start | bytes 393220
  18.8 247.2 %copy-start.4 = (f32[10,1024]{1,0:T(8,128)S(1)}, f32[10,1024]{1,0:T(8,128)}, u32[]{:S(2)}) copy-start(f32[10,1024]{1,0:T(8,128)} %param.15) | copy-start | bytes 122884
  18.8 247.1 %copy-start.5 = (f32[10,1024]{1,0:T(8,128)S(1)}, f32[10,1024]{1,0:T(8,128)}, u32[]{:S(2)}) copy-start(f32[10,1024]{1,0:T(8,128)} %param.16) | copy-start | bytes 122884
  18.8 247.1 %copy-start.6 = (f32[10,1024]{1,0:T(8,128)S(1)}, f32[10,1024]{1,0:T(8,128)}, u32[]{:S(2)}) copy-start(f32[10,1024]{1,0:T(8,128)} %param.17) | copy-start | bytes 122884
  18.8 320.2 %all-gather.2.cloned.1.call-start = ((), (), s32[]{:S(2)}) async-start(), calls=%async_computation.2 | async-start | bytes 4259840 | tf_op jit(solution)/shard_map/all_gather | solution.py:70
Sparse Core Ops, SparseCore 0:
  18.9 150.4 reduce-scatter.1
  263.7 75.2 all-gather.1

commit v2 on v0

--- a/solution.py
+++ b/solution.py
@@ -3,6 +3,7 @@
 import jax.numpy as jnp
 from jax import lax
 from jax.sharding import PartitionSpec as P
+from jax.lax import all_to_all, axis_size
 
 D = 4096
 EXPERTS = 8
@@ -66,7 +67,15 @@
         small_gradient, scale, small_first, small_second, small_master, row_decay
     )
     owned_weights = master_new.astype(jnp.bfloat16)
-    gathered = lax.all_gather(owned_weights, ("shard", "section"), axis=0, tiled=True)
+    gathered = jnp.concatenate(
+        all_to_all(
+            jnp.stack([owned_weights] * axis_size(("shard", "section"))),
+            axis_name=("shard", "section"),
+            split_axis=0,
+            concat_axis=0,
+        ),
+        0,
+    )
     return (
         master_new,
         first_new,

time: 455 us -> 486 us (1.068)
  waiting for transfers between devices: 72 us -> 93.2 us
  starting transfers between devices: 0.08 us -> 7.01 us
    all_to_all x0 -> x1, waiting for transfers between devices: none -> 93.2 us  [body(): all_to_all(jnp.stack([owned_weights] * axis_size(('shard', 'section'))),...]
    all_gather x1 -> x0, waiting for transfers between devices: 72 us -> none  [body(): lax.all_gather(owned_weights, ('shard', 'section'), axis=0, tiled=True)]
    all_to_all x0 -> x1, starting transfers between devices: none -> 6.97 us  [body(): all_to_all(jnp.stack([owned_weights] * axis_size(('shard', 'section'))),...]
    another operation x0 -> x1, local copies, waits for them, and re-layouts: none -> 6.06 us  [body(): jnp.stack([owned_weights] * axis_size(('shard', 'section')))]
where the time goes in v2:
time: 486 us; the launch traced here: 485 us
  blocking collectives  337 us (69%)
  waiting for transfers between devices  93.2 us (19%)
  local copies, waits for them, and re-layouts  18 us (4%)
  between operations  15.5 us (3%)
  matrix products  10.3 us (2%)
  starting transfers between devices  7.01 us (1%)
    psum x1, blocking collectives, body(): small_gradient = lax.psum(local_small, ('shard', 'section'))  247 us
    all_to_all x1, waiting for transfers between devices, body(): all_to_all(jnp.stack([owned_weights] * axis_size(('shard', 'section'))),...  93.2 us
    psum x1, blocking collectives, body(): big_total = lax.psum(owned_squares, ('shard', 'tensor', 'section'))  81.1 us
    unnamed x20, local copies, waits for them, and re-layouts  11.9 us
    dot_general x1, matrix products, body(): jnp.einsum('tf,tjc->fjc', normed_inputs, projection_cotangent, preferred_...  10.3 us
  transfers between devices with their start and end apart: 2, of which 1 were waited for; matrix products, arithmetic and copies ran while one was open for 1% of the time, Pallas kernels for 0%

profile of v2, /device:TPU:1, one launch (start us, length us, event | category | flops | bytes accessed | tf_op | source)
XLA Modules:
  0.0 485.4 jit_solution(16180263967471010232)
XLA Ops:
  7.2 0.0 copy-start
  7.2 0.0 reduce-scatter.2.cloned.1.call-start
  7.2 1.2 copy-done
  8.4 10.3 %fusion = f32[4096,2,256]{2,0,1:T(8,128)} fusion(bf16[1024,4096]{1,0:T(8,128)(2,1)} %param.9, bf16[1024,2,256]{2,1,0:T(2,128)(2,1)S(1)} %copy-done), kind=kOutput, calls=%fused_computation | convolution fusion | flops 4294967296 | bytes 17825792 | tf_op jit(solution)/shard_map/tf,tjc->fjc/dot_general | solution.py:45
  18.8 0.0 reduce-scatter.2.cloned.1.call-update
  18.8 0.7 copy-done.7
  19.5 246.9 %psum.22 = f32[10,1024]{1,0:T(8,128)S(1)} all-reduce(f32[10,1024]{1,0:T(8,128)S(1)} %bitcast_convert_fusion), channel_id=1, replica_groups=mesh['shard'=8,'tensor'=4,'section'=8] {'shard','section'}, use_global_device_ids=true, to_apply=%region_3.0 | all-reduce | flops 10240 | bytes 81920 | tf_op jit(solution)/shard_map/psum | solution.py:54
  266.4 0.6 multiply_reduce_fusion.1
  267.1 1.5 multiply_reduce_fusion
  268.6 9.4 %psum.23 = f32[]{:T(128)} all-reduce(f32[]{:T(128)} %multiply_reduce_fusion.1), channel_id=1, replica_groups=mesh['shard'=8,'tensor'=4,'section'=8] {'tensor'}, use_global_device_ids=true, to_apply=%region_5.0 | all-reduce | flops 1 | bytes 8 | tf_op jit(solution)/shard_map/psum | solution.py:56
  278.0 81.1 %psum.21 = f32[]{:T(128)} all-reduce(f32[]{:T(128)} %multiply_reduce_fusion), channel_id=1, replica_groups=mesh['shard'=8,'tensor'=4,'section'=8] {'shard','tensor','section'}, use_global_device_ids=true, to_apply=%region_2.0 | all-reduce | flops 1 | bytes 8 | tf_op jit(solution)/shard_map/psum | solution.py:55
  360.5 0.0 copy-done.1
  360.5 1.0 fusion.8
  361.6 0.1 copy.23
  361.6 6.1 %stack.2 = bf16[64,64,2,256]{3,2,1,0:T(2,128)(2,1)} broadcast(bf16[64,2,256]{2,1,0:T(2,128)(2,1)S(1)} %copy.23), dimensions={1,2,3} | broadcast | bytes 4259840 | tf_op jit(solution)/shard_map/stack | solution.py:72
  367.7 7.0 %all-to-all-start = ((bf16[64,64,2,256]{3,2,1,0:T(2,128)(2,1)}), bf16[64,64,2,256]{3,2,1,0:T(2,128)(2,1)}, u32[]{:S(2)}, u32[]{:S(2)}) async-start(bf16[64,64,2,256]{3,2,1,0:T(2,128)(2,1)} %stack.2), calls=%async_computation.1 | async-start | bytes 8388608 | tf_op jit(solution)/shard_map/all_to_all | solution.py:71
  374.7 0.8 copy.24
  375.5 0.8 copy.25
  376.2 0.8 copy.26
  377.0 0.0 copy-done.4
  377.0 0.0 copy-done.6
  377.0 0.7 fusion.6
  377.7 93.2 %all-to-all-done = bf16[64,64,2,256]{3,2,1,0:T(2,128)(2,1)} async-done(((bf16[64,64,2,256]{3,2,1,0:T(2,128)(2,1)}), bf16[64,64,2,256]{3,2,1,0:T(2,128)(2,1)}, u32[]{:S(2)}, u32[]{:S(2)}) %all-to-all-start) | async-done | bytes 4194336 | tf_op jit(solution)/shard_map/all_to_all | solution.py:71
  470.9 7.7 %copy.42 = bf16[4096,2,256]{2,1,0:T(2,128)(2,1)} copy(bf16[4096,2,256]{2,1,0:T(2,128)(2,1)} %bitcast.2) | data formatting | bytes 8388608
  (13 shorter events, 0.0 us)
Async XLA Ops:
  7.2 1.2 copy-start
  7.2 259.9 %reduce-scatter.2.cloned.1.call-start = ((), (), s32[]{:S(2)}) async-start(), calls=%async_computation.2 | async-start | bytes 8519680 | tf_op jit(solution)/shard_map/reduce_scatter | solution.py:44
  18.7 0.8 copy-start.7
  18.7 341.8 %copy-start.1 = (f32[64,2,256]{2,1,0:T(2,128)S(1)}, f32[64,2,256]{2,1,0:T(2,128)}, u32[]{:S(2)}) copy-start(f32[64,2,256]{2,1,0:T(2,128)} %param.12) | copy-start | bytes 393220
  18.7 341.8 %copy-start.2 = (f32[64,2,256]{2,1,0:T(2,128)S(1)}, f32[64,2,256]{2,1,0:T(2,128)}, u32[]{:S(2)}) copy-start(f32[64,2,256]{2,1,0:T(2,128)} %param.13) | copy-start | bytes 393220
  18.8 341.8 %copy-start.3 = (f32[64,2,256]{2,1,0:T(2,128)S(1)}, f32[64,2,256]{2,1,0:T(2,128)}, u32[]{:S(2)}) copy-start(f32[64,2,256]{2,1,0:T(2,128)} %param.14) | copy-start | bytes 393220
  19.5 357.5 %copy-start.4 = (f32[10,1024]{1,0:T(8,128)S(1)}, f32[10,1024]{1,0:T(8,128)}, u32[]{:S(2)}) copy-start(f32[10,1024]{1,0:T(8,128)} %param.15) | copy-start | bytes 122884
  19.5 357.5 %copy-start.5 = (f32[10,1024]{1,0:T(8,128)S(1)}, f32[10,1024]{1,0:T(8,128)}, u32[]{:S(2)}) copy-start(f32[10,1024]{1,0:T(8,128)} %param.16) | copy-start | bytes 122884
  19.5 357.5 %copy-start.6 = (f32[10,1024]{1,0:T(8,128)S(1)}, f32[10,1024]{1,0:T(8,128)}, u32[]{:S(2)}) copy-start(f32[10,1024]{1,0:T(8,128)} %param.17) | copy-start | bytes 122884
  367.7 103.2 %all-to-all-start = ((bf16[64,64,2,256]{3,2,1,0:T(2,128)(2,1)}), bf16[64,64,2,256]{3,2,1,0:T(2,128)(2,1)}, u32[]{:S(2)}, u32[]{:S(2)}) async-start(bf16[64,64,2,256]{3,2,1,0:T(2,128)(2,1)} %stack.2), calls=%async_computation.1 | async-start | bytes 8388608 | tf_op jit(solution)/shard_map/all_to_all | solution.py:71
Sparse Core Ops, SparseCore 0:
  18.9 150.7 reduce-scatter.1
